TPU v7x, 32 devices: a whole 2x2x4 slice. The times are simulated.
32 devices in a mesh: dp: 8 (over z, y), tensor: 4 (over x, core).
Axes of the slice: x: 2, y: 2, z: 4, core: 2. Of those that a mesh axis runs over, the one named last changes fastest.
Arguments:
- tokens: bfloat16 [12288, 768], P('dp', 'tensor'), may hold values from -6 to 6
- cotangent: bfloat16 [12288, 768], P('dp', 'tensor'), may hold values from -6 to 6
- seq_start: int32 [12288], P('dp'), may hold values from 0 to 384, as said below
- row_place: int32 [8, 1536], P('dp'), may hold values from 0 to 1535, each once within a row
- qkv_weight: bfloat16 [3, 768, 768], P(None, None, 'tensor'), may hold values from -0.21875 to 0.21875
- qv_bias: bfloat16 [2, 768], P(None, 'tensor'), may hold values from -1.5 to 1.5
- out_weight: bfloat16 [768, 768], P('tensor'), may hold values from -0.875 to 0.875
- out_bias: bfloat16 [768], replicated, may hold values from -1.5 to 1.5
- first_gain: bfloat16 [768], replicated, may hold values from 0.5 to 1.5
- first_shift: bfloat16 [768], replicated, may hold values from -1.5 to 1.5
- up_weight: bfloat16 [2, 768, 3072], P(None, None, 'tensor'), may hold values from -0.21875 to 0.21875
- up_bias: bfloat16 [2, 3072], P(None, 'tensor'), may hold values from -1.5 to 1.5
- down_weight: bfloat16 [3072, 768], P('tensor'), may hold values from -0.15625 to 0.15625
- down_bias: bfloat16 [768], replicated, may hold values from -1.5 to 1.5
- second_gain: bfloat16 [768], replicated, may hold values from 0.5 to 1.5
- second_shift: bfloat16 [768], replicated, may hold values from -1.5 to 1.5
Outputs:
- layer_out: bfloat16 [12288, 768], P('dp', 'tensor')
- input_grad: bfloat16 [12288, 768], P('dp', 'tensor')
- qkv_grad: float32 [3, 768, 768], P(None, 'dp', 'tensor')
- qv_bias_grad: float32 [2, 768], P(None, 'tensor')
- out_grad: float32 [768, 768], P('tensor', 'dp')
- out_bias_grad: float32 [768], P('dp')
- first_gain_grad: float32 [768], P('dp')
- first_shift_grad: float32 [768], P('dp')
- up_grad: float32 [2, 768, 3072], P(None, 'dp', 'tensor')
- up_bias_grad: float32 [2, 3072], P(None, 'tensor')
- down_grad: float32 [3072, 768], P('tensor', 'dp')
- down_bias_grad: float32 [768], P('dp')
- second_gain_grad: float32 [768], P('dp')
- second_shift_grad: float32 [768], P('dp')
Inputs may be any that keep to these rules, and one draw needn't show every extreme that they name: seq_start of a token is the offset, within its aligned block of 512 packed rows, of the first token of its sequence; sequences are 128, 256 or 512 tokens long, begin at multiples of 128 and never cross a block. Each row of row_place is a permutation of 0 to 1535.
All inputs are finite; a program needn't handle non-finite values.
Results may differ from a plain program's by a relative error of at most 0.02.
The roundings to bfloat16 on the way count: a program that leaves them out, or rounds other values in their place, can miss the bound.
Values may be sent and summed in bfloat16 or wider, within the bound.
A program may use at most 128 MiB of HBM per device.

v0:
```python
import jax
import jax.numpy as jnp
from jax import lax
from jax.sharding import PartitionSpec as P

HEADS = 12
HEAD_DIM = 64
BLOCK = 512


def layer_norm(values, scale_row, shift_row):
    center = values - jnp.mean(values, axis=-1, keepdims=True)
    spread = jnp.mean(center * center, axis=-1, keepdims=True)
    return center * lax.rsqrt(spread + 1e-05) * scale_row + shift_row


def gated_unit(gate_part, value_part):
    return jax.nn.gelu(gate_part, approximate=False) * value_part


def alibi_terms(part_index, local_heads, block_rows):
    heads_idx = (part_index * local_heads + jnp.arange(local_heads)).astype(jnp.float32)
    slopes = 2.0 ** (-8.0 * (heads_idx + 1.0) / HEADS)
    position = jnp.arange(block_rows).astype(jnp.float32)
    distance = jnp.abs(position[:, None] - position[None, :])
    return -slopes[:, None, None] * distance[None]


def block_scores(queries, key_rows, alibi_bias, same_seq, score_scale):
    raw_scores = jnp.einsum(
        "bqhe,bkhe->bhqk", queries, key_rows, preferred_element_type=jnp.float32
    )
    scored = raw_scores * score_scale + alibi_bias[None]
    return jnp.where(same_seq[:, None], scored, -1e30)


def softmax_rows(scored):
    row_max = jnp.max(scored, axis=-1, keepdims=True)
    exponent = jnp.exp(scored - row_max)
    denominator = jnp.sum(exponent, axis=-1, keepdims=True)
    return (exponent / denominator, row_max + jnp.log(denominator))


def on_device(
    tokens,
    cotangent,
    seq_start,
    row_place,
    qkv_weight,
    qv_bias,
    out_weight,
    out_bias,
    first_gain,
    first_shift,
    up_weight,
    up_bias,
    down_weight,
    down_bias,
    second_gain,
    second_shift,
):
    arr_tokens, arr_cot = (
        lax.all_to_all(tokens, "dp", split_axis=0, concat_axis=0, tiled=True),
        lax.all_to_all(cotangent, "dp", split_axis=0, concat_axis=0, tiled=True),
    )
    wide_tokens, wide_cot = (
        lax.all_gather(arr_tokens, "tensor", axis=1, tiled=True),
        lax.all_gather(arr_cot, "tensor", axis=1, tiled=True),
    )
    slot_index = row_place[0]
    packed_in = jnp.zeros_like(wide_tokens).at[slot_index].set(wide_tokens)
    packed_cot = jnp.zeros_like(wide_cot).at[slot_index].set(wide_cot)
    row_count = packed_in.shape[0]
    columns = packed_in.shape[1]
    local_heads = qkv_weight.shape[2] // HEAD_DIM
    block_rows = BLOCK
    blocks = row_count // block_rows
    part_index = lax.axis_index("tensor")
    col_count = columns // lax.axis_size("tensor")
    score_scale = HEAD_DIM ** (-0.5)
    alibi_bias = alibi_terms(part_index, local_heads, block_rows)
    block_starts = seq_start.reshape(blocks, block_rows)
    same_seq = block_starts[:, :, None] == block_starts[:, None, :]
    bias_rows = jnp.stack([qv_bias[0], jnp.zeros_like(qv_bias[0]), qv_bias[1]]).astype(jnp.float32)
    projected = jnp.einsum("td,kde->kte", packed_in, qkv_weight, preferred_element_type=jnp.float32)
    qkv_rows = (projected + bias_rows[:, None, :]).astype(jnp.bfloat16)
    split_heads = qkv_rows.reshape(3, blocks, block_rows, local_heads, HEAD_DIM)
    queries = split_heads[0]
    key_rows = split_heads[1]
    value_rows = split_heads[2]
    attn_probs, log_total = softmax_rows(
        block_scores(queries, key_rows, alibi_bias, same_seq, score_scale)
    )
    context = jnp.einsum(
        "bhqk,bkhe->bqhe",
        attn_probs.astype(jnp.bfloat16),
        value_rows,
        preferred_element_type=jnp.float32,
    )
    context = context.reshape(row_count, local_heads * HEAD_DIM).astype(jnp.bfloat16)
    attn_part = jnp.dot(context, out_weight, preferred_element_type=jnp.float32)
    attended = lax.psum(attn_part, "tensor")
    hidden = packed_in.astype(jnp.float32) + (attended + out_bias.astype(jnp.float32))
    normed, first_pull = jax.vjp(
        layer_norm, hidden, first_gain.astype(jnp.float32), first_shift.astype(jnp.float32)
    )
    normed_low = normed.astype(jnp.bfloat16)
    lifted = jnp.einsum("td,kdf->ktf", normed_low, up_weight, preferred_element_type=jnp.float32)
    lifted = lifted + up_bias.astype(jnp.float32)[:, None, :]
    gated_val, gate_pull = jax.vjp(gated_unit, lifted[0], lifted[1])
    gated_low = gated_val.astype(jnp.bfloat16)
    ffn_part = jnp.dot(gated_low, down_weight, preferred_element_type=jnp.float32)
    ffn_out = lax.psum(ffn_part.astype(jnp.bfloat16), "tensor").astype(jnp.float32)
    mixed_rows = normed + (ffn_out + down_bias.astype(jnp.float32))
    result, second_pull = jax.vjp(
        layer_norm, mixed_rows, second_gain.astype(jnp.float32), second_shift.astype(jnp.float32)
    )
    grad_scale = (row_count * lax.axis_size("dp")) ** (-0.5)
    d_mixed, d_second_gain, d_second_shift = second_pull(packed_cot.astype(jnp.float32))
    d_mixed_low = d_mixed.astype(jnp.bfloat16)
    g_down = jnp.einsum("tf,td->fd", gated_low, d_mixed_low, preferred_element_type=jnp.float32)
    g_down_bias = jnp.sum(d_mixed, axis=0)
    d_gated = jnp.einsum("td,fd->tf", d_mixed_low, down_weight, preferred_element_type=jnp.float32)
    d_gate, d_value = gate_pull(d_gated)
    d_lifted = jnp.stack([d_gate, d_value]).astype(jnp.bfloat16)
    g_up = jnp.einsum("td,ktf->kdf", normed_low, d_lifted, preferred_element_type=jnp.float32)
    g_up_bias = jnp.sum(d_lifted, axis=1, dtype=jnp.float32)
    d_normed_part = jnp.einsum(
        "ktf,kdf->td", d_lifted, up_weight, preferred_element_type=jnp.float32
    )
    d_normed = d_mixed + lax.psum(d_normed_part.astype(jnp.bfloat16), "tensor").astype(jnp.float32)
    d_hidden, d_first_gain, d_first_shift = first_pull(d_normed)
    d_hidden_low = d_hidden.astype(jnp.bfloat16)
    g_out = jnp.einsum("te,td->ed", context, d_hidden_low, preferred_element_type=jnp.float32)
    g_out_bias = jnp.sum(d_hidden, axis=0)
    d_context = jnp.einsum(
        "td,ed->te", d_hidden_low, out_weight, preferred_element_type=jnp.float32
    )
    d_context = d_context.astype(jnp.bfloat16).reshape(blocks, block_rows, local_heads, HEAD_DIM)
    probs_back = jnp.exp(
        block_scores(queries, key_rows, alibi_bias, same_seq, score_scale) - log_total
    )
    d_probs = jnp.einsum(
        "bqhe,bkhe->bhqk", d_context, value_rows, preferred_element_type=jnp.float32
    )
    g_values = jnp.einsum(
        "bhqk,bqhe->bkhe",
        probs_back.astype(jnp.bfloat16),
        d_context,
        preferred_element_type=jnp.float32,
    )
    center_term = jnp.sum(probs_back * d_probs, axis=-1, keepdims=True)
    d_scores = (probs_back * (d_probs - center_term)).astype(jnp.bfloat16)
    g_queries = (
        jnp.einsum("bhqk,bkhe->bqhe", d_scores, key_rows, preferred_element_type=jnp.float32)
        * score_scale
    )
    g_keys = (
        jnp.einsum("bhqk,bqhe->bkhe", d_scores, queries, preferred_element_type=jnp.float32)
        * score_scale
    )
    d_qkv = jnp.stack([g_queries, g_keys, g_values]).reshape(3, row_count, local_heads * HEAD_DIM)
    d_qkv = d_qkv.astype(jnp.bfloat16)
    g_qkv = jnp.einsum("td,kte->kde", packed_in, d_qkv, preferred_element_type=jnp.float32)
    g_qv_bias = jnp.sum(jnp.stack([d_qkv[0], d_qkv[2]]), axis=1, dtype=jnp.float32)
    d_input_part = jnp.einsum("kte,kde->td", d_qkv, qkv_weight, preferred_element_type=jnp.float32)
    hidden_cols = lax.dynamic_slice_in_dim(d_hidden, part_index * col_count, col_count, 1)
    grad_cols = hidden_cols + lax.psum_scatter(
        d_input_part.astype(jnp.bfloat16), "tensor", scatter_dimension=1, tiled=True
    ).astype(jnp.float32)
    summed = (
        lax.psum_scatter(g_qkv * grad_scale, "dp", scatter_dimension=1, tiled=True),
        lax.psum_scatter(g_out * grad_scale, "dp", scatter_dimension=1, tiled=True),
        lax.psum_scatter(g_out_bias * grad_scale, "dp", scatter_dimension=0, tiled=True),
        lax.psum_scatter(d_first_gain * grad_scale, "dp", scatter_dimension=0, tiled=True),
        lax.psum_scatter(d_first_shift * grad_scale, "dp", scatter_dimension=0, tiled=True),
        lax.psum_scatter(g_up * grad_scale, "dp", scatter_dimension=1, tiled=True),
        lax.psum_scatter(g_down * grad_scale, "dp", scatter_dimension=1, tiled=True),
        lax.psum_scatter(g_down_bias * grad_scale, "dp", scatter_dimension=0, tiled=True),
        lax.psum_scatter(d_second_gain * grad_scale, "dp", scatter_dimension=0, tiled=True),
        lax.psum_scatter(d_second_shift * grad_scale, "dp", scatter_dimension=0, tiled=True),
    )
    qkv_grad, out_grad, out_bias_grad, first_gain_grad, first_shift_grad = (
        summed[0],
        summed[1],
        summed[2],
        summed[3],
        summed[4],
    )
    up_grad, down_grad, down_bias_grad, second_gain_grad, second_shift_grad = (
        summed[5],
        summed[6],
        summed[7],
        summed[8],
        summed[9],
    )
    qv_bias_grad, up_bias_grad = lax.psum((g_qv_bias * grad_scale, g_up_bias * grad_scale), "dp")
    layer_cols = lax.dynamic_slice_in_dim(result, part_index * col_count, col_count, 1)
    layer_back = layer_cols[slot_index].astype(jnp.bfloat16)
    grad_back = grad_cols[slot_index].astype(jnp.bfloat16)
    layer_out, input_grad = (
        lax.all_to_all(layer_back, "dp", split_axis=0, concat_axis=0, tiled=True),
        lax.all_to_all(grad_back, "dp", split_axis=0, concat_axis=0, tiled=True),
    )
    return (
        layer_out,
        input_grad,
        qkv_grad,
        qv_bias_grad,
        out_grad,
        out_bias_grad,
        first_gain_grad,
        first_shift_grad,
        up_grad,
        up_bias_grad,
        down_grad,
        down_bias_grad,
        second_gain_grad,
        second_shift_grad,
    )


def solution(mesh):
    return jax.shard_map(
        on_device,
        mesh=mesh,
        in_specs=(
            P("dp", "tensor"),
            P("dp", "tensor"),
            P("dp"),
            P("dp", None),
            P(None, None, "tensor"),
            P(None, "tensor"),
            P("tensor", None),
            P(),
            P(),
            P(),
            P(None, None, "tensor"),
            P(None, "tensor"),
            P("tensor", None),
            P(),
            P(),
            P(),
        ),
        out_specs=(
            P("dp", "tensor"),
            P("dp", "tensor"),
            P(None, "dp", "tensor"),
            P(None, "tensor"),
            P("tensor", "dp"),
            P("dp"),
            P("dp"),
            P("dp"),
            P(None, "dp", "tensor"),
            P(None, "tensor"),
            P("tensor", "dp"),
            P("dp"),
            P("dp"),
            P("dp"),
        ),
        check_vma=False,
    )
```

profile of v0, /device:TPU:0, one launch (start us, length us, event | category | flops | bytes accessed | tf_op | source)
XLA Modules:
  0.0 849.5 jit_solution(2268085062084630268)
XLA Ops:
  9.3 27.3 %all_to_all.42 = bf16[8,192,192]{1,2,0:T(8,128)(2,1)S(1)} all-to-all(bf16[8,192,192]{1,2,0:T(8,128)(2,1)S(1)} %copy.124), channel_id=1, replica_groups=mesh['dp'=8,'tensor'=4] {'dp'}, dimensions={0} | all-to-all | bytes 1179648 | tf_op jit(solution)/shard_map/all_to_all | solution.py:63
  42.5 19.2 %all-gather.3.cloned.1.call-done = bf16[1536,768]{0,1:T(8,128)(2,1)} async-done(((bf16[1536,192]{0,1:T(8,128)(2,1)}), bf16[1536,768]{0,1:T(8,128)(2,1)}) %all-gather.3.cloned.1.call-update) | async-done | bytes 2359312 | tf_op jit(solution)/shard_map/all_gather | solution.py:67
  66.0 10.1 %scatter_custom_fusion = bf16[1536,768]{1,0:T(8,128)(2,1)} fusion(s32[1536]{0:T(1024)S(1)} %fusion.70, bf16[1536,768]{1,0:T(8,128)(2,1)} %copy.126, bf16[]{:T(256)} %constant.46.clone.1), kind=kCustom, calls=%fused_computation.108 | custom fusion | bytes 2359808 | tf_op jit(solution)/shard_map/scatter | solution.py:71
  103.5 5.5 all-to-all-start.2
  109.2 20.5 %all-to-all-done.2 = bf16[8,192,192]{1,2,0:T(8,128)(2,1)} async-done(((bf16[8,192,192]{1,2,0:T(8,128)(2,1)}), bf16[8,192,192]{1,2,0:T(8,128)(2,1)}, u32[]{:S(2)}, u32[]{:S(2)}) %all-to-all-start.2) | async-done | bytes 589856 | tf_op jit(solution)/shard_map/all_to_all | solution.py:64
  134.9 58.2 %all-reduce.13.cloned.1.call-done = f32[1536,768]{1,0:T(8,128)} async-done(((f32[1536,768]{1,0:T(8,128)}), f32[1536,768]{1,0:T(8,128)}) %all-reduce.13.cloned.1.call-update) | async-done | bytes 4718608 | tf_op jit(solution)/shard_map/psum | solution.py:102
  201.9 11.5 %multiply_convert_fusion.2 = (bf16[1536,768]{1,0:T(8,128)(2,1)S(1)}, f32[1536,768]{1,0:T(8,128)}) fusion(f32[2,1536,768]{2,1,0:T(8,128)S(1)} %add_bitcast_fusion), kind=kLoop, calls=%fused_computation.51 | loop fusion | flops 77856768 | bytes 16515072 | tf_op jit(solution)/shard_map/convert_element_type | solution.py:111
  223.7 9.8 %scatter_custom_fusion.1 = bf16[1536,768]{1,0:T(8,128)(2,1)} fusion(s32[1536]{0:T(1024)} %copy-done.29, bf16[1536,768]{1,0:T(8,128)(2,1)} %copy.135, bf16[]{:T(256)} %constant.46.clone.1), kind=kCustom, calls=%fused_computation.106 | custom fusion | bytes 2359808 | tf_op jit(solution)/shard_map/scatter | solution.py:72
  233.6 43.8 %all-reduce.15.cloned.1.call-done = bf16[1536,768]{1,0:T(8,128)(2,1)} async-done(((bf16[1536,768]{1,0:T(8,128)(2,1)}), bf16[1536,768]{1,0:T(8,128)(2,1)}) %all-reduce.15.cloned.1.call-update) | async-done | bytes 2359312 | tf_op jit(solution)/shard_map/psum | solution.py:113
  289.2 7.1 fusion.36
  297.7 7.0 bitcast_convert_fusion.1
  305.8 54.8 %all-reduce.17.cloned.1.call-done = bf16[1536,768]{1,0:T(8,128)(2,1)} async-done(((bf16[1536,768]{1,0:T(8,128)(2,1)}), bf16[1536,768]{1,0:T(8,128)(2,1)}) %all-reduce.17.cloned.1.call-update) | async-done | bytes 2359312 | tf_op jit(solution)/shard_map/psum | solution.py:131
  360.6 6.5 multiply_reduce_fusion.1
  382.2 7.2 multiply_reduce_fusion
  389.4 11.2 %multiply_convert_fusion = bf16[3,3,512,512]{2,3,1,0:T(8,128)(2,1)} fusion(f32[3,3,512,512]{2,3,1,0:T(8,128)} %get-tuple-element.127, f32[3,3,512,512]{2,3,1,0:T(8,128)} %copy-done.2, f32[3,3,512]{2,1,0:T(4,128)S(1)} %get-tuple-element.126, f32[3,3,512]{2,1,0:T(4,128)S(1)} %copy-done.23), kind=kLoop, calls=%fused_computation.5 | loop fusion | flops 9437184 | bytes 23629824 | tf_op jit(solution)/shard_map/convert_element_type | solution.py:153
  439.8 9.6 %multiply_bitcast_fusion = f32[2,768,768]{1,2,0:T(8,128)} fusion(bf16[1,1536,768]{2,1,0:T(8,128)(2,1)} %get-tuple-element.114, bf16[1,1536,768]{2,1,0:T(8,128)(2,1)S(1)} %copy-done.19, f32[1536,768]{1,0:T(8,128)} %copy-done.3, f32[768]{0:T(1024)S(1)} %copy-done.34, f32[768]{0:T(1024)S(1)} %copy-done.28, f32[1536]{0:T(1024)S(1)} %fusion.68, ...), kind=kOutput, calls=%fused_computation.43 | convolution fusion | flops 3633315840 | bytes 14174208 | tf_op jit(solution)/shard_map/td,ktf->kdf/dot_general | solution.py:126
  449.4 8.3 copy.150
  459.3 6.0 convolution_multiply_fusion
  467.7 5.4 gather_fusion
  482.7 17.3 %all-to-all-done.1 = bf16[8,192,192]{2,1,0:T(8,128)(2,1)S(1)} async-done(((bf16[8,192,192]{2,1,0:T(8,128)(2,1)}), bf16[8,192,192]{2,1,0:T(8,128)(2,1)S(1)}, u32[]{:S(2)}, u32[]{:S(2)}) %all-to-all-start.1) | async-done | bytes 589856 | tf_op jit(solution)/shard_map/all_to_all | solution.py:202
  515.3 44.6 %all-reduce.7 = (f32[2,192]{1,0:T(2,128)}, f32[768]{0:T(1024)S(1)}, f32[768]{0:T(1024)S(1)}, f32[768]{0:T(1024)S(1)}, f32[2,768]{1,0:T(2,128)}, /*index=5*/f32[7...) all-reduce(f32[2,192]{1,0:T(2,128)S(1)} %broadcast_multiply_fusion.10, ...), channel_id=1, replica_groups=mesh['dp'=8,'tensor'=4] {'dp'}, use_global_device_ids=true, to_apply=%region_19.20 | all-reduce | flops 6528 | bytes 52224 | tf_op jit(solution)/shard_map/psum | solution.py:197
  565.0 32.5 %reduce-scatter.15.cloned.1.call-done = f32[96,576]{1,0:T(8,128)} async-done(((f32[768,576]{1,0:T(8,128)}), f32[96,576]{1,0:T(8,128)}) %reduce-scatter.15.cloned.1.call-update) | async-done | bytes 221200
  599.4 170.4 %all-reduce.19.cloned.1.call-done = f32[2,768,768]{2,0,1:T(2,128)} async-done(((f32[2,768,768]{2,0,1:T(2,128)}), f32[2,768,768]{2,0,1:T(2,128)}) %all-reduce.19.cloned.1.call-update) | async-done | bytes 4718608
  772.8 69.6 %reduce-scatter.11.cloned.1.call-done = f32[768,96]{0,1:T(8,128)} async-done(((f32[768,768]{0,1:T(8,128)}), f32[768,96]{0,1:T(8,128)}) %reduce-scatter.11.cloned.1.call-update) | async-done | bytes 294928 | tf_op jit(solution)/shard_map/reduce_scatter | solution.py:178
  (248 shorter events, 170.1 us)
Async XLA Ops:
  7.2 190.4 %copy-start = (bf16[2,768,768]{2,1,0:T(8,128)(2,1)S(1)}, bf16[2,768,768]{2,1,0:T(8,128)(2,1)}, u32[]{:S(2)}) copy-start(bf16[2,768,768]{2,1,0:T(8,128)(2,1)} %param.26) | copy-start | bytes 7077892
  7.2 31.4 %copy-start.39 = (s32[1536]{0:T(1024)S(1)}, s32[1536]{0:T(1024)}, u32[]{:S(2)}) copy-start(s32[1536]{0:T(1024)} %param.18) | copy-start | bytes 18436
  7.2 31.5 %copy-start.40 = (s32[1,1536]{1,0:T(1,128)S(1)}, s32[1,1536]{1,0:T(1,128)}, u32[]{:S(2)}) copy-start(s32[1,1536]{1,0:T(1,128)} %param.19) | copy-start | bytes 18436
  7.2 31.5 %copy-start.43 = (bf16[2,192]{1,0:T(2,128)(2,1)S(1)}, bf16[2,192]{1,0:T(2,128)(2,1)}, u32[]{:S(2)}) copy-start(bf16[2,192]{1,0:T(2,128)(2,1)} %param.21) | copy-start | bytes 2308
  7.2 54.5 %all-gather.3.cloned.1.call-start = ((), (), s32[]{:S(2)}) async-start(), calls=%async_computation.8 | async-start | bytes 2949120 | tf_op jit(solution)/shard_map/all_gather | solution.py:67
  38.5 154.5 %all-reduce.13.cloned.1.call-start = ((), (), s32[]{:S(2)}) async-start(), calls=%async_computation.9 | async-start | bytes 9437184 | tf_op jit(solution)/shard_map/psum | solution.py:102
  38.8 27.3 %copy-start.29 = (s32[1536]{0:T(1024)}, s32[1536]{0:T(1024)S(1)}, u32[]{:S(2)}) copy-start(s32[1536]{0:T(1024)S(1)} %fusion.70) | copy-start | bytes 18436
  40.4 35.7 %copy-start.51 = (bf16[3,768,192]{1,2,0:T(8,128)(2,1)S(1)}, bf16[3,768,192]{1,2,0:T(8,128)(2,1)}, u32[]{:S(2)}) copy-start(bf16[3,768,192]{1,2,0:T(8,128)(2,1)} %param.20) | copy-start | bytes 2654212
  103.5 26.2 %all-to-all-start.2 = ((bf16[8,192,192]{1,2,0:T(8,128)(2,1)}), bf16[8,192,192]{1,2,0:T(8,128)(2,1)}, u32[]{:S(2)}, u32[]{:S(2)}) async-start(bf16[8,192,192]{1,2,0:T(8,128)(2,1)} %copy.133), calls=%async_computation.2 | async-start | bytes 1572864 | tf_op jit(solution)/shard_map/all_to_all | solution.py:64
  109.1 110.4 %all-gather.5.cloned.1.call-start = ((), (), s32[]{:S(2)}) async-start(), calls=%async_computation.11 | async-start | bytes 2949120 | tf_op jit(solution)/shard_map/all_gather | solution.py:68
  109.1 258.0 %copy-start.27 = (f32[768]{0:T(1024)}, f32[768]{0:T(1024)S(1)}, u32[]{:S(2)}) copy-start(f32[768]{0:T(1024)S(1)} %convert_element_type.142) | copy-start | bytes 9220
  109.2 168.2 %copy-start.33 = (f32[768]{0:T(1024)}, f32[768]{0:T(1024)S(1)}, u32[]{:S(2)}) copy-start(f32[768]{0:T(1024)S(1)} %convert_element_type.143) | copy-start | bytes 9220
  134.7 142.7 %all-reduce.15.cloned.1.call-start = ((), (), s32[]{:S(2)}) async-start(), calls=%async_computation.10 | async-start | bytes 4718592 | tf_op jit(solution)/shard_map/psum | solution.py:113
  218.4 142.2 %all-reduce.17.cloned.1.call-start = ((), (), s32[]{:S(2)}) async-start(), calls=%async_computation.12 | async-start | bytes 4718592 | tf_op jit(solution)/shard_map/psum | solution.py:131
  289.1 78.0 %copy-start.25 = (f32[1536]{0:T(1024)}, f32[1536]{0:T(1024)S(1)}, u32[]{:S(2)}) copy-start(f32[1536]{0:T(1024)S(1)} %negate_multiply_fusion.2) | copy-start | bytes 18436
  304.7 196.4 %reduce-scatter.13.cloned.1.call-start = ((), (), s32[]{:S(2)}) async-start(), calls=%async_computation.14 | async-start | bytes 2949120
  407.9 13.8 %copy-start.13 = (bf16[1,1536,192]{1,2,0:T(8,128)(2,1)}, bf16[1,1536,192]{1,2,0:T(8,128)(2,1)S(1)}, u32[]{:S(2)}) copy-start(bf16[1,1536,192]{1,2,0:T(8,128)(2,1)S(1)} %stack.36) | copy-start | bytes 1769476
  421.7 141.7 %reduce-scatter.17.cloned.1.call-start = ((), (), s32[]{:S(2)}) async-start(), calls=%async_computation.16 | async-start | bytes 884736
  426.0 171.4 %reduce-scatter.15.cloned.1.call-start = ((), (), s32[]{:S(2)}) async-start(), calls=%async_computation.15 | async-start | bytes 2211840
  439.7 330.1 %all-reduce.19.cloned.1.call-start = ((), (), s32[]{:S(2)}) async-start(), calls=%async_computation.17 | async-start | bytes 9437184
  457.7 384.7 %reduce-scatter.11.cloned.1.call-start = ((), (), s32[]{:S(2)}) async-start(), calls=%async_computation.13 | async-start | bytes 2654208 | tf_op jit(solution)/shard_map/reduce_scatter | solution.py:178
  473.0 27.0 %all-to-all-start.1 = ((bf16[8,192,192]{2,1,0:T(8,128)(2,1)}), bf16[8,192,192]{2,1,0:T(8,128)(2,1)S(1)}, u32[]{:S(2)}, u32[]{:S(2)}) async-start(bf16[8,192,192]{2,1,0:T(8,128)(2,1)} %bitcast.11), calls=%async_computation.1 | async-start | bytes 1572864 | tf_op jit(solution)/shard_map/all_to_all | solution.py:202
  504.7 337.7 %copy-start.1 = (bf16[2,768,768]{2,1,0:T(8,128)(2,1)S(1)}, bf16[2,768,768]{2,1,0:T(8,128)(2,1)}, u32[]{:S(2)}) copy-start(bf16[2,768,768]{2,1,0:T(8,128)(2,1)} %param.26) | copy-start | bytes 7077892
  510.0 261.7 %all-to-all-start.3 = ((bf16[8,192,192]{2,1,0:T(8,128)(2,1)}), bf16[8,192,192]{2,1,0:T(8,128)(2,1)S(1)}, u32[]{:S(2)}, u32[]{:S(2)}) async-start(bf16[8,192,192]{2,1,0:T(8,128)(2,1)} %bitcast.200), calls=%async_computation.3 | async-start | bytes 1572864 | tf_op jit(solution)/shard_map/all_to_all | solution.py:203
  (47 other events, 305.2 us)
Sparse Core Ops, SparseCore 0:
  38.7 23.0 all-gather.2
  99.0 94.0 all-reduce.12
  195.2 24.1 all-gather.4
  221.7 55.6 all-reduce.14
  304.8 55.7 all-reduce.16
  421.8 32.8 reduce-scatter.12
  458.0 66.9 reduce-scatter.16
  528.5 68.9 reduce-scatter.14
  601.1 168.6 all-reduce.18
  773.7 68.6 reduce-scatter.10
where the time goes:
time: 856 us; the launch traced here: 849 us
  waiting for transfers between devices  487 us (57%)
  local copies, waits for them, and re-layouts  110 us (13%)
  matrix products  82.2 us (10%)
  blocking collectives  71.8 us (8%)
  other arithmetic  66.4 us (8%)
  between operations  16.1 us (2%)
  starting transfers between devices  15.7 us (2%)
    unnamed x14, waiting for transfers between devices  203 us
    reduce_scatter x1, waiting for transfers between devices, on_device(): lax.psum_scatter(g_down * grad_scale, 'dp', scatter_dimension=1, tiled=True)  69.6 us
    psum x1, waiting for transfers between devices, on_device(): attended = lax.psum(attn_part, 'tensor')  58.2 us
    psum x1, waiting for transfers between devices, on_device(): lax.psum(d_normed_part.astype(jnp.bfloat16), 'tensor').astype(jnp.float32)  54.8 us
    psum x1, blocking collectives, on_device(): lax.psum((g_qv_bias * grad_scale, g_up_bias * grad_scale), 'dp')  44.6 us
    psum x1, waiting for transfers between devices, on_device(): lax.psum(ffn_part.astype(jnp.bfloat16), 'tensor').astype(jnp.float32)  43.8 us
    unnamed x135, local copies, waits for them, and re-layouts  31.6 us
    all_to_all x1, blocking collectives, on_device(): lax.all_to_all(tokens, 'dp', split_axis=0, concat_axis=0, tiled=True)  27.3 us
  transfers between devices with their start and end apart: 13, of which 10 were waited for; matrix products, arithmetic and copies ran while one was open for 14% of the time, Pallas kernels for 0%

commit v1 on v0

--- a/solution.py
+++ b/solution.py
@@ -99,7 +99,11 @@
     )
     context = context.reshape(row_count, local_heads * HEAD_DIM).astype(jnp.bfloat16)
     attn_part = jnp.dot(context, out_weight, preferred_element_type=jnp.float32)
-    attended = lax.psum(attn_part, "tensor")
+    attended = attn_part
+    for hop in (1, 2):
+        attended = attended + lax.ppermute(
+            attended, "tensor", [(dev, dev ^ hop) for dev in range(4)]
+        )
     hidden = packed_in.astype(jnp.float32) + (attended + out_bias.astype(jnp.float32))
     normed, first_pull = jax.vjp(
         layer_norm, hidden, first_gain.astype(jnp.float32), first_shift.astype(jnp.float32)

time: 856 us -> 889 us (1.039)
  waiting for transfers between devices: 487 us -> 507 us
  local copies, waits for them, and re-layouts: 110 us -> 121 us
    ppermute x0 -> x2, waiting for transfers between devices: none -> 84.2 us  [on_device(): lax.ppermute(attended, 'tensor', [(dev, dev ^ hop) for dev in range(4)])]
    psum x1 -> x0, waiting for transfers between devices: 58.2 us -> none  [on_device(): attended = lax.psum(attn_part, 'tensor')]
    unnamed x135 -> x130, local copies, waits for them, and re-layouts: 31.6 us -> 33.7 us
    unnamed x14 -> x12, waiting for transfers between devices: 203 us -> 204 us
  transfers between devices with their start and end apart: 13 -> 14, of which waited for: 10 -> 10; matrix products, arithmetic and copies ran while one was open for 14% -> 15% of each run, Pallas kernels for 0% -> 0%
where the time goes in v1:
time: 889 us; the launch traced here: 882 us
  waiting for transfers between devices  507 us (57%)
  local copies, waits for them, and re-layouts  121 us (14%)
  blocking collectives  74.9 us (8%)
  matrix products  73.8 us (8%)
  other arithmetic  72.8 us (8%)
  starting transfers between devices  16.7 us (2%)
  between operations  15.9 us (2%)
    unnamed x12, waiting for transfers between devices  204 us
    ppermute x2, waiting for transfers between devices, on_device(): lax.ppermute(attended, 'tensor', [(dev, dev ^ hop) for dev in range(4)])  84.2 us
    reduce_scatter x1, waiting for transfers between devices, on_device(): lax.psum_scatter(g_down * grad_scale, 'dp', scatter_dimension=1, tiled=True)  69.6 us
    psum x1, waiting for transfers between devices, on_device(): lax.psum(d_normed_part.astype(jnp.bfloat16), 'tensor').astype(jnp.float32)  55.8 us
    psum x1, blocking collectives, on_device(): lax.psum((g_qv_bias * grad_scale, g_up_bias * grad_scale), 'dp')  47.6 us
    psum x1, waiting for transfers between devices, on_device(): lax.psum(ffn_part.astype(jnp.bfloat16), 'tensor').astype(jnp.float32)  36.8 us
    unnamed x130, local copies, waits for them, and re-layouts  33.7 us
    all_to_all x1, blocking collectives, on_device(): lax.all_to_all(tokens, 'dp', split_axis=0, concat_axis=0, tiled=True)  27.3 us
  transfers between devices with their start and end apart: 14, of which 10 were waited for; matrix products, arithmetic and copies ran while one was open for 15% of the time, Pallas kernels for 0%

profile of v1, /device:TPU:0, one launch (start us, length us, event | category | flops | bytes accessed | tf_op | source)
XLA Modules:
  0.0 881.7 jit_solution(14229800986557239957)
XLA Ops:
  9.3 27.3 %all_to_all.42 = bf16[8,192,192]{1,2,0:T(8,128)(2,1)S(1)} all-to-all(bf16[8,192,192]{1,2,0:T(8,128)(2,1)S(1)} %copy.118), channel_id=1, replica_groups=mesh['dp'=8,'tensor'=4] {'dp'}, dimensions={0} | all-to-all | bytes 1179648 | tf_op jit(solution)/shard_map/all_to_all | solution.py:63
  42.5 19.3 %all-gather.3.cloned.1.call-done = bf16[1536,768]{0,1:T(8,128)(2,1)} async-done(((bf16[1536,192]{0,1:T(8,128)(2,1)}), bf16[1536,768]{0,1:T(8,128)(2,1)}) %all-gather.3.cloned.1.call-update) | async-done | bytes 2359312 | tf_op jit(solution)/shard_map/all_gather | solution.py:67
  66.0 9.8 %scatter_custom_fusion = bf16[1536,768]{1,0:T(8,128)(2,1)} fusion(s32[1536]{0:T(1024)S(1)} %fusion.70, bf16[1536,768]{1,0:T(8,128)(2,1)} %copy.120, bf16[]{:T(256)} %constant.46.clone.1), kind=kCustom, calls=%fused_computation.107 | custom fusion | bytes 2359808 | tf_op jit(solution)/shard_map/scatter | solution.py:71
  96.8 7.7 collective-permute-done
  112.6 5.7 all-to-all-start.2
  118.7 20.1 %all-to-all-done.2 = bf16[8,192,192]{1,2,0:T(8,128)(2,1)} async-done(((bf16[8,192,192]{1,2,0:T(8,128)(2,1)}), bf16[8,192,192]{1,2,0:T(8,128)(2,1)}, u32[]{:S(2)}, u32[]{:S(2)}) %all-to-all-start.2) | async-done | bytes 589856 | tf_op jit(solution)/shard_map/all_to_all | solution.py:64
  148.0 76.5 %collective-permute-done.1 = f32[1536,768]{0,1:T(8,128)} collective-permute-done((f32[1536,768]{0,1:T(8,128)}, f32[1536,768]{0,1:T(8,128)}, u32[]{:S(2)}, u32[]{:S(2)}) %collective-permute-start.1) | collective-permute-done | bytes 4718624 | tf_op jit(solution)/shard_map/ppermute | solution.py:104
  235.0 11.5 %multiply_convert_fusion.2 = (bf16[1536,768]{1,0:T(8,128)(2,1)S(1)}, f32[1536,768]{1,0:T(8,128)}) fusion(f32[2,1536,768]{2,1,0:T(8,128)S(1)} %add_bitcast_fusion), kind=kLoop, calls=%fused_computation.51 | loop fusion | flops 77856768 | bytes 16515072 | tf_op jit(solution)/shard_map/convert_element_type | solution.py:115
  256.3 9.8 %scatter_custom_fusion.1 = bf16[1536,768]{1,0:T(8,128)(2,1)} fusion(s32[1536]{0:T(1024)} %copy-done.27, bf16[1536,768]{1,0:T(8,128)(2,1)} %copy.133, bf16[]{:T(256)} %constant.46.clone.1), kind=kCustom, calls=%fused_computation.105 | custom fusion | bytes 2359808 | tf_op jit(solution)/shard_map/scatter | solution.py:72
  270.4 36.8 %all-reduce.12.cloned.1.call-done = bf16[1536,768]{0,1:T(8,128)(2,1)} async-done(((bf16[1536,768]{0,1:T(8,128)(2,1)}), bf16[1536,768]{0,1:T(8,128)(2,1)}) %all-reduce.12.cloned.1.call-update) | async-done | bytes 2359312 | tf_op jit(solution)/shard_map/psum | solution.py:117
  332.3 55.8 %all-reduce.14.cloned.1.call-done = bf16[1536,768]{0,1:T(8,128)(2,1)} async-done(((bf16[1536,768]{0,1:T(8,128)(2,1)}), bf16[1536,768]{0,1:T(8,128)(2,1)}) %all-reduce.14.cloned.1.call-update) | async-done | bytes 2359312 | tf_op jit(solution)/shard_map/psum | solution.py:135
  388.1 6.2 fusion.76
  411.7 7.2 multiply_reduce_fusion
  418.9 11.2 %multiply_convert_fusion = bf16[3,3,512,512]{2,3,1,0:T(8,128)(2,1)} fusion(f32[3,3,512,512]{2,3,1,0:T(8,128)} %get-tuple-element.113, f32[3,3,512,512]{2,3,1,0:T(8,128)} %copy-done.2, f32[3,3,512]{2,1,0:T(4,128)S(1)} %get-tuple-element.112, f32[3,3,512]{2,1,0:T(4,128)S(1)} %log_add_fusion), kind=kLoop, calls=%fused_computation.5 | loop fusion | flops 9437184 | bytes 23629824 | tf_op jit(solution)/shard_map/convert_element_type | solution.py:157
  456.0 10.4 %multiply_bitcast_fusion = f32[2,768,768]{1,2,0:T(8,128)} fusion(bf16[1,1536,768]{2,1,0:T(8,128)(2,1)} %copy-done.11, bf16[1,1536,768]{2,1,0:T(8,128)(2,1)S(1)} %copy-done.10, f32[1536,768]{0,1:T(8,128)} %copy-done.3, f32[768]{0:T(1024)} %copy-done.30, f32[768]{0:T(1024)} %copy-done.24, f32[1536]{0:T(1024)S(1)} %fusion.68, ...), kind=kOutput, calls=%fused_computation.43 | convolution fusion | flops 3633315840 | bytes 14174208 | tf_op jit(solution)/shard_map/td,ktf->kdf/dot_general | solution.py:130
  466.4 8.3 copy.151
  490.1 5.8 convolution_multiply_fusion
  497.8 5.4 gather_fusion
  503.2 5.4 all-to-all-start.1
  513.0 16.8 %all-to-all-done.1 = bf16[8,192,192]{2,1,0:T(8,128)(2,1)S(1)} async-done(((bf16[8,192,192]{2,1,0:T(8,128)(2,1)}), bf16[8,192,192]{2,1,0:T(8,128)(2,1)S(1)}, u32[]{:S(2)}, u32[]{:S(2)}) %all-to-all-start.1) | async-done | bytes 589856 | tf_op jit(solution)/shard_map/all_to_all | solution.py:206
  543.4 47.6 %all-reduce.7 = (f32[2,192]{1,0:T(2,128)}, f32[768]{0:T(1024)S(1)}, f32[768]{0:T(1024)S(1)}, f32[768]{0:T(1024)S(1)}, f32[2,768]{1,0:T(2,128)}, /*index=5*/f32[7...) all-reduce(f32[2,192]{1,0:T(2,128)S(1)} %broadcast_multiply_fusion.10, ...), channel_id=1, replica_groups=mesh['dp'=8,'tensor'=4] {'dp'}, use_global_device_ids=true, to_apply=%region_18.19 | all-reduce | flops 6528 | bytes 52224 | tf_op jit(solution)/shard_map/psum | solution.py:201
  596.1 136.0 %all-reduce.16.cloned.1.call-done = f32[2,768,768]{2,0,1:T(2,128)} async-done(((f32[2,768,768]{2,0,1:T(2,128)}), f32[2,768,768]{2,0,1:T(2,128)}) %all-reduce.16.cloned.1.call-update) | async-done | bytes 4718608
  734.0 68.0 %reduce-scatter.13.cloned.1.call-done = f32[96,576]{1,0:T(8,128)} async-done(((f32[768,576]{1,0:T(8,128)}), f32[96,576]{1,0:T(8,128)}) %reduce-scatter.13.cloned.1.call-update) | async-done | bytes 221200
  805.0 69.6 %reduce-scatter.11.cloned.1.call-done = f32[768,96]{0,1:T(8,128)} async-done(((f32[768,768]{0,1:T(8,128)}), f32[768,96]{0,1:T(8,128)}) %reduce-scatter.11.cloned.1.call-update) | async-done | bytes 294928 | tf_op jit(solution)/shard_map/reduce_scatter | solution.py:182
  (250 shorter events, 187.5 us)
Async XLA Ops:
  7.2 223.3 %copy-start = (bf16[2,768,768]{2,1,0:T(8,128)(2,1)S(1)}, bf16[2,768,768]{2,1,0:T(8,128)(2,1)}, u32[]{:S(2)}) copy-start(bf16[2,768,768]{2,1,0:T(8,128)(2,1)} %param.26) | copy-start | bytes 7077892
  7.2 31.4 %copy-start.36 = (s32[1536]{0:T(1024)S(1)}, s32[1536]{0:T(1024)}, u32[]{:S(2)}) copy-start(s32[1536]{0:T(1024)} %param.18) | copy-start | bytes 18436
  7.2 31.5 %copy-start.37 = (s32[1,1536]{1,0:T(1,128)S(1)}, s32[1,1536]{1,0:T(1,128)}, u32[]{:S(2)}) copy-start(s32[1,1536]{1,0:T(1,128)} %param.19) | copy-start | bytes 18436
  7.2 31.5 %copy-start.40 = (bf16[2,192]{1,0:T(2,128)(2,1)S(1)}, bf16[2,192]{1,0:T(2,128)(2,1)}, u32[]{:S(2)}) copy-start(bf16[2,192]{1,0:T(2,128)(2,1)} %param.21) | copy-start | bytes 2308
  7.2 54.5 %all-gather.3.cloned.1.call-start = ((), (), s32[]{:S(2)}) async-start(), calls=%async_computation.8 | async-start | bytes 2949120 | tf_op jit(solution)/shard_map/all_gather | solution.py:67
  38.7 27.3 %copy-start.27 = (s32[1536]{0:T(1024)}, s32[1536]{0:T(1024)S(1)}, u32[]{:S(2)}) copy-start(s32[1536]{0:T(1024)S(1)} %fusion.70) | copy-start | bytes 18436
  40.3 35.5 %copy-start.49 = (bf16[3,768,192]{1,2,0:T(8,128)(2,1)S(1)}, bf16[3,768,192]{1,2,0:T(8,128)(2,1)}, u32[]{:S(2)}) copy-start(bf16[3,768,192]{1,2,0:T(8,128)(2,1)} %param.20) | copy-start | bytes 2654212
  96.5 8.0 collective-permute-start
  107.7 116.9 %collective-permute-start.1 = (f32[1536,768]{0,1:T(8,128)}, f32[1536,768]{0,1:T(8,128)}, u32[]{:S(2)}, u32[]{:S(2)}) collective-permute-start(f32[1536,768]{0,1:T(8,128)} %add.182), channel_id=1, source_target_pairs={{0,2},{1,3},{2,0},{3,1},{4,6},{5,7},{6,4},{7,5},{8,10},{9,11},{10,... | collective-permute-start | bytes 14155784 | tf_op jit(solution)/shard_map/ppermute | solution.py:104
  112.6 26.1 %all-to-all-start.2 = ((bf16[8,192,192]{1,2,0:T(8,128)(2,1)}), bf16[8,192,192]{1,2,0:T(8,128)(2,1)}, u32[]{:S(2)}, u32[]{:S(2)}) async-start(bf16[8,192,192]{1,2,0:T(8,128)(2,1)} %copy.131), calls=%async_computation.2 | async-start | bytes 1572864 | tf_op jit(solution)/shard_map/all_to_all | solution.py:64
  118.3 133.7 %all-gather.5.cloned.1.call-start = ((), (), s32[]{:S(2)}) async-start(), calls=%async_computation.10 | async-start | bytes 2949120 | tf_op jit(solution)/shard_map/all_gather | solution.py:68
  118.6 280.1 %copy-start.24 = (f32[768]{0:T(1024)}, f32[768]{0:T(1024)S(1)}, u32[]{:S(2)}) copy-start(f32[768]{0:T(1024)S(1)} %convert_element_type.142) | copy-start | bytes 9220
  118.7 188.6 %copy-start.30 = (f32[768]{0:T(1024)}, f32[768]{0:T(1024)S(1)}, u32[]{:S(2)}) copy-start(f32[768]{0:T(1024)S(1)} %convert_element_type.143) | copy-start | bytes 9220
  143.7 163.6 %all-reduce.12.cloned.1.call-start = ((), (), s32[]{:S(2)}) async-start(), calls=%async_computation.9 | async-start | bytes 4718592 | tf_op jit(solution)/shard_map/psum | solution.py:117
  251.5 136.7 %all-reduce.14.cloned.1.call-start = ((), (), s32[]{:S(2)}) async-start(), calls=%async_computation.11 | async-start | bytes 4718592 | tf_op jit(solution)/shard_map/psum | solution.py:135
  317.9 70.2 %copy-start.25 = (f32[1536]{0:T(1024)}, f32[1536]{0:T(1024)S(1)}, u32[]{:S(2)}) copy-start(f32[1536]{0:T(1024)S(1)} %negate_multiply_fusion.2) | copy-start | bytes 18436
  332.2 198.6 %reduce-scatter.9.cloned.1.call-start = ((), (), s32[]{:S(2)}) async-start(), calls=%async_computation.12 | async-start | bytes 2949120 | tf_op jit(solution)/shard_map/reduce_scatter | solution.py:172
  451.2 143.2 %reduce-scatter.15.cloned.1.call-start = ((), (), s32[]{:S(2)}) async-start(), calls=%async_computation.15 | async-start | bytes 884736
  455.9 276.1 %all-reduce.16.cloned.1.call-start = ((), (), s32[]{:S(2)}) async-start(), calls=%async_computation.16 | async-start | bytes 9437184
  474.7 327.4 %reduce-scatter.13.cloned.1.call-start = ((), (), s32[]{:S(2)}) async-start(), calls=%async_computation.14 | async-start | bytes 2211840
  489.8 384.9 %reduce-scatter.11.cloned.1.call-start = ((), (), s32[]{:S(2)}) async-start(), calls=%async_computation.13 | async-start | bytes 2654208 | tf_op jit(solution)/shard_map/reduce_scatter | solution.py:182
  503.2 26.6 %all-to-all-start.1 = ((bf16[8,192,192]{2,1,0:T(8,128)(2,1)}), bf16[8,192,192]{2,1,0:T(8,128)(2,1)S(1)}, u32[]{:S(2)}, u32[]{:S(2)}) async-start(bf16[8,192,192]{2,1,0:T(8,128)(2,1)} %bitcast.11), calls=%async_computation.1 | async-start | bytes 1572864 | tf_op jit(solution)/shard_map/all_to_all | solution.py:206
  532.8 341.9 %copy-start.1 = (bf16[2,768,768]{2,1,0:T(8,128)(2,1)S(1)}, bf16[2,768,768]{2,1,0:T(8,128)(2,1)}, u32[]{:S(2)}) copy-start(bf16[2,768,768]{2,1,0:T(8,128)(2,1)} %param.26) | copy-start | bytes 7077892
  538.1 265.8 %all-to-all-start.3 = ((bf16[8,192,192]{2,1,0:T(8,128)(2,1)}), bf16[8,192,192]{2,1,0:T(8,128)(2,1)S(1)}, u32[]{:S(2)}, u32[]{:S(2)}) async-start(bf16[8,192,192]{2,1,0:T(8,128)(2,1)} %bitcast.196), calls=%async_computation.4 | async-start | bytes 1572864 | tf_op jit(solution)/shard_map/all_to_all | solution.py:207
  (46 other events, 351.4 us)
Sparse Core Ops, SparseCore 0:
  38.7 23.0 all-gather.2
  143.8 35.7 all-gather.4
  251.6 55.6 all-reduce.11
  332.4 55.7 all-reduce.13
  451.3 32.8 reduce-scatter.8
  487.4 68.3 reduce-scatter.14
  559.4 172.6 all-reduce.15
  735.5 66.4 reduce-scatter.12
  806.2 68.4 reduce-scatter.10
